TPU v7x, 256 devices: a whole 4x4x8 slice. The times are simulated.
256 devices in a mesh: req: 32 (over y, x, core), head: 8 (over z).
Axes of the slice: x: 4, y: 4, z: 8, core: 2. Of those that a mesh axis runs over, the one named last changes fastest.
Arguments:
- queries: bfloat16 [1024, 16384], P(('req', 'head')), may hold values from -15 to 15
- cache_keys: bfloat16 [8, 32768, 1024], P(None, 'req', 'head'), may hold values from -6 to 6
- cache_values: bfloat16 [8, 32768, 1024], P(None, 'req', 'head'), may hold values from -6 to 6
- tree_keys: bfloat16 [1024, 1024], P('req', 'head'), may hold values from -10 to 10
- tree_values: bfloat16 [1024, 1024], P('req', 'head'), may hold values from -6 to 6
- parents: int32 [8, 128], replicated, may hold values from -1 to 126, as said below
- tree_sizes: int32 [8], replicated, may hold values from 16 to 128
- cache_lens: int32 [8], replicated, may hold values from 2 to 32768
Outputs:
- attended: bfloat16 [1024, 16384], P('req', 'head')
Inputs may be any that keep to these rules, and one draw needn't show every extreme that they name: parents[a, 0] = -1 (the root); for node i >= 1, parents[a, i] is a node of 0 to i - 1.
All inputs are finite; a program needn't handle non-finite values.
Results may differ from a plain program's by a relative error of at most 0.003.
Values may be sent and summed in bfloat16 or wider, within the bound.
A program may use at most 128 MiB of HBM per device.

v0:
```python
import math
import jax
import jax.numpy as jnp
from jax import lax
from jax.sharding import Mesh
from jax.sharding import PartitionSpec as P

NH = 128
KVH = 8
HD = 128
negative_fill = -1e30


def ancestry(parents):
    node_count = parents.shape[1]
    node_ids = jnp.arange(node_count, dtype=jnp.int32)
    linked = jnp.logical_or(
        parents[:, :, None] == node_ids[None, None, :], node_ids[:, None] == node_ids[None, :]
    )
    reached = linked.astype(jnp.bfloat16)
    for doubling in range((node_count - 1).bit_length()):
        squared = jnp.einsum("aij,ajk->aik", reached, reached, preferred_element_type=jnp.float32)
        reached = jnp.minimum(squared, 1.0).astype(jnp.bfloat16)
    return reached


def body(
    queries, cache_keys, cache_values, tree_keys, tree_values, parents, tree_sizes, cache_lens
):
    group_size = NH // KVH
    softmax_scale = 1.0 / math.sqrt(HD)
    request = lax.axis_index("rh")
    quarter = lax.axis_index("rl")
    n_lo = lax.axis_size("rl")
    n_hi = lax.axis_size("rh")
    cache_block = cache_keys.shape[1]
    kv_local = cache_keys.shape[2] // HD
    heads_local = kv_local * group_size
    node_count = parents.shape[1]
    rows_owned = tree_keys.shape[0]
    by_head = lax.all_to_all(queries, "head", split_axis=1, concat_axis=0, tiled=True)
    query_block = lax.all_gather(by_head, "rl", axis=0, tiled=True)
    query_block = query_block.reshape(node_count, kv_local, group_size, HD)
    both = jnp.concatenate([cache_keys, cache_values], axis=2)
    mine = lax.all_to_all(both, "rh", split_axis=0, concat_axis=1, tiled=True)[0]
    mine = mine.reshape(n_hi, cache_block, 2, kv_local, HD)
    reached = ancestry(parents)
    ancestors = lax.dynamic_index_in_dim(reached, request, 0, keepdims=False)
    ancestors = lax.dynamic_slice_in_dim(ancestors, quarter * rows_owned, rows_owned, 1)
    live_tree_all = ancestors > 0.5
    length = lax.dynamic_index_in_dim(cache_lens, request, 0, keepdims=False)
    local_tree_keys = tree_keys.reshape(rows_owned, kv_local, HD)
    local_tree_values = tree_values.reshape(rows_owned, kv_local, HD)

    def one_group(s):
        block = s * n_lo + quarter
        positions = block * cache_block + jnp.arange(cache_block, dtype=jnp.int32)
        live_cache = positions < length
        live_tree = jnp.logical_and(live_tree_all, s == request)
        block_keys = mine[s, :, 0]
        block_values = mine[s, :, 1]
        cache_scores = (
            jnp.einsum(
                "igqd,pgd->igqp", query_block, block_keys, preferred_element_type=jnp.float32
            )
            * softmax_scale
        )
        cache_scores = jnp.where(live_cache[None, None, None, :], cache_scores, negative_fill)
        tree_scores = (
            jnp.einsum(
                "igqd,rgd->igqr", query_block, local_tree_keys, preferred_element_type=jnp.float32
            )
            * softmax_scale
        )
        tree_scores = jnp.where(live_tree[:, None, None, :], tree_scores, negative_fill)
        peaks = jnp.maximum(jnp.max(cache_scores, axis=3), jnp.max(tree_scores, axis=3))
        cache_weights = jnp.where(
            live_cache[None, None, None, :], jnp.exp(cache_scores - peaks[..., None]), 0.0
        )
        tree_weights = jnp.where(
            live_tree[:, None, None, :], jnp.exp(tree_scores - peaks[..., None]), 0.0
        )
        totals = jnp.sum(cache_weights, axis=3) + jnp.sum(tree_weights, axis=3)
        group_sums = jnp.einsum(
            "igqp,pgd->igqd",
            cache_weights.astype(jnp.bfloat16),
            block_values,
            preferred_element_type=jnp.float32,
        )
        group_sums = group_sums + jnp.einsum(
            "igqr,rgd->igqd",
            tree_weights.astype(jnp.bfloat16),
            local_tree_values,
            preferred_element_type=jnp.float32,
        )
        floored = jnp.maximum(totals, 1.0)
        partial_value = group_sums / floored[..., None]
        log_total = peaks + jnp.log(floored)
        return (
            partial_value.reshape(node_count, heads_local, HD),
            log_total.reshape(node_count, heads_local),
        )

    partials, log_totals = lax.map(one_group, jnp.arange(n_hi, dtype=jnp.int32))
    top = jnp.max(log_totals, axis=0)
    weights = jnp.exp(log_totals - top)
    den = jnp.sum(weights, axis=0)
    acc = jnp.sum(weights[..., None] * partials, axis=0)
    payload = jnp.concatenate(
        [acc.reshape(node_count, heads_local * HD), den, top], axis=1
    ).reshape(n_lo, rows_owned, heads_local * HD + 2 * heads_local)
    gathered = lax.all_to_all(payload, "rl", split_axis=0, concat_axis=0, tiled=True)
    got_acc = gathered[:, :, : heads_local * HD].reshape(n_lo, rows_owned, heads_local, HD)
    got_den = gathered[:, :, heads_local * HD : heads_local * HD + heads_local]
    got_top = gathered[:, :, heads_local * HD + heads_local :]
    highest = jnp.max(got_top, axis=0)
    scale = jnp.exp(got_top - highest)
    num = jnp.sum(scale[..., None] * got_acc, axis=0)
    total = jnp.sum(scale * got_den, axis=0)
    merged = (num / total[..., None]).reshape(rows_owned, heads_local * HD)
    row_nodes = quarter * rows_owned + jnp.arange(rows_owned, dtype=jnp.int32)
    live_size = lax.dynamic_index_in_dim(tree_sizes, request, 0, keepdims=False)
    live_rows = row_nodes < live_size
    return jnp.where(live_rows[:, None], merged, 0.0).astype(jnp.bfloat16)


def solution(mesh):

    def run(
        queries, cache_keys, cache_values, tree_keys, tree_values, parents, tree_sizes, cache_lens
    ):
        n_hi = cache_keys.shape[0]
        n_lo = mesh.shape["req"] // n_hi
        split = Mesh(mesh.devices.reshape(n_hi, n_lo, mesh.shape["head"]), ("rh", "rl", "head"))
        rows = ("rh", "rl")
        placed = (
            P(("rh", "rl", "head"), None),
            P(None, rows, "head"),
            P(None, rows, "head"),
            P(rows, "head"),
            P(rows, "head"),
            P(),
            P(),
            P(),
        )
        return jax.shard_map(
            body, mesh=split, in_specs=placed, out_specs=P(rows, "head"), check_vma=False
        )(
            queries,
            cache_keys,
            cache_values,
            tree_keys,
            tree_values,
            parents,
            tree_sizes,
            cache_lens,
        )

    return run
```

profile of v0, /device:TPU:1, one launch (start us, length us, event | category | flops | bytes accessed | tf_op | source)
XLA Modules:
  0.0 273.4 jit_solution(10835699050133776124)
XLA Ops:
  0.0 9.1 %all-to-all-start.1 = ((bf16[4,8,2048]{2,0,1:T(4,128)(2,1)}), bf16[4,8,2048]{2,0,1:T(4,128)(2,1)S(1)}, u32[]{:S(2)}, u32[]{:S(2)}) async-start(bf16[4,8,2048]{2,0,1:T(4,128)(2,1)} %bitcast.168), calls=%async_computation.1 | async-start | bytes 262144 | tf_op jit(solution)/shard_map/all_to_all | solution.py:41
  20.2 6.7 %all-to-all-start = ((bf16[8,1024,256]{1,2,0:T(8,128)(2,1)}), bf16[8,1024,256]{1,2,0:T(8,128)(2,1)}, u32[]{:S(2)}, u32[]{:S(2)}) async-start(bf16[8,1024,256]{1,2,0:T(8,128)(2,1)} %pad_maximum_fusion), calls=%async_computation | async-start | bytes 8388608 | tf_op jit(solution)/shard_map/all_to_all | solution.py:45
  29.7 47.9 %all_gather.3 = bf16[128,2048]{1,0:T(8,128)(2,1)S(1)} all-gather(bf16[32,2048]{1,0:T(8,128)(2,1)S(1)} %all_to_all.28), channel_id=1, replica_groups=mesh['rh'=8,'rl'=4,'head'=8] {'rl'}, dimensions={0}, use_global_device_ids=true | all-gather | bytes 655360 | tf_op jit(solution)/shard_map/all_gather | solution.py:42
  78.5 6.5 %copy.69 = bf16[8,1024,2,1,128]{4,1,3,2,0:T(8,128)(2,1)} copy(bf16[8,1024,2,1,128]{1,4,2,0,3:T(8,128)(2,1)} %bitcast.20) | data formatting | bytes 8388608 | tf_op jit(solution)/shard_map/while | solution.py:104
  85.0 160.4 %while.14 = (s32[]{:T(128)}, f32[8,128,16,128]{1,3,2,0:T(8,128)}, f32[8,128,16]{1,2,0:T(8,128)S(1)}, s32[8]{0:T(128)S(1)}, bf16[8,1024,2,1,128]{4,1,3,2,0:T(8,12...) while((s32[]{:T(128)}, f32[8,128,16,128]{1,3,2,0:T(8,128)}, ...), condition=%wide.region_5.6_spmd, body=%wide.region_0.5_spmd.sunk | while | flops 1119164416 | bytes 55485768 | solution.py:104
  88.9 5.5 %bitcast_reduce_fusion.2 = (f32[128,16]{0,1:T(8,128)S(1)}, f32[1024,128,16]{1,0,2:T(8,128)}) fusion(pred[1024]{0:T(1024)(128)(4,1)S(1)} %add_compare_fusion.3, bf16[128,1,16,128]{3,0,2,1:T(8,128)(2,1)S(1)} %get-tuple-element.349, bf16[8,1024,2,1,128]{4,1,3,2,0:T(8,128)(2,1)} %get-tuple-element.346, s32[]{:T(128)S(6)} %select_n.118), kind=kOutput, calls=%fused_computation.1.clone.1 | convolution fusion | flops 543160320 | bytes 9184260 | tf_op jit(solution)/shard_map/while/body/eval_jaxpr/igqd,pgd->igqp/dot_general | solution.py:63
  95.2 5.8 %fusion.85 = f32[128,128,16]{1,0,2:T(8,128)S(1)} fusion(f32[1024,128,16]{1,0,2:T(8,128)} %get-tuple-element.304, f32[128,16]{0,1:T(8,128)S(1)} %max.47, pred[1024]{0:T(1024)(128)(4,1)S(1)} %add_compare_fusion.3, bf16[8,1024,2,1,128]{4,1,3,2,0:T(8,128)(2,1)} %get-tuple-element.346, s32[]{:T(128)S(6)} %select_n.118), kind=kOutput, calls=%fused_computation.8.clone.1 | convolution fusion | flops 547356672 | bytes 9709572 | tf_op jit(solution)/shard_map/while/body/eval_jaxpr/igqp,pgd->igqd/dot_general | solution.py:84
  108.9 5.5 %bitcast_reduce_fusion.2 = (f32[128,16]{0,1:T(8,128)S(1)}, f32[1024,128,16]{1,0,2:T(8,128)}) fusion(pred[1024]{0:T(1024)(128)(4,1)S(1)} %add_compare_fusion.3, bf16[128,1,16,128]{3,0,2,1:T(8,128)(2,1)S(1)} %get-tuple-element.349, bf16[8,1024,2,1,128]{4,1,3,2,0:T(8,128)(2,1)} %get-tuple-element.346, s32[]{:T(128)S(6)} %select_n.118), kind=kOutput, calls=%fused_computation.1.clone.1 | convolution fusion | flops 543160320 | bytes 9184260 | tf_op jit(solution)/shard_map/while/body/eval_jaxpr/igqd,pgd->igqp/dot_general | solution.py:63
  115.2 5.8 %fusion.85 = f32[128,128,16]{1,0,2:T(8,128)S(1)} fusion(f32[1024,128,16]{1,0,2:T(8,128)} %get-tuple-element.304, f32[128,16]{0,1:T(8,128)S(1)} %max.47, pred[1024]{0:T(1024)(128)(4,1)S(1)} %add_compare_fusion.3, bf16[8,1024,2,1,128]{4,1,3,2,0:T(8,128)(2,1)} %get-tuple-element.346, s32[]{:T(128)S(6)} %select_n.118), kind=kOutput, calls=%fused_computation.8.clone.1 | convolution fusion | flops 547356672 | bytes 9709572 | tf_op jit(solution)/shard_map/while/body/eval_jaxpr/igqp,pgd->igqd/dot_general | solution.py:84
  129.0 5.5 %bitcast_reduce_fusion.2 = (f32[128,16]{0,1:T(8,128)S(1)}, f32[1024,128,16]{1,0,2:T(8,128)}) fusion(pred[1024]{0:T(1024)(128)(4,1)S(1)} %add_compare_fusion.3, bf16[128,1,16,128]{3,0,2,1:T(8,128)(2,1)S(1)} %get-tuple-element.349, bf16[8,1024,2,1,128]{4,1,3,2,0:T(8,128)(2,1)} %get-tuple-element.346, s32[]{:T(128)S(6)} %select_n.118), kind=kOutput, calls=%fused_computation.1.clone.1 | convolution fusion | flops 543160320 | bytes 9184260 | tf_op jit(solution)/shard_map/while/body/eval_jaxpr/igqd,pgd->igqp/dot_general | solution.py:63
  135.3 5.8 %fusion.85 = f32[128,128,16]{1,0,2:T(8,128)S(1)} fusion(f32[1024,128,16]{1,0,2:T(8,128)} %get-tuple-element.304, f32[128,16]{0,1:T(8,128)S(1)} %max.47, pred[1024]{0:T(1024)(128)(4,1)S(1)} %add_compare_fusion.3, bf16[8,1024,2,1,128]{4,1,3,2,0:T(8,128)(2,1)} %get-tuple-element.346, s32[]{:T(128)S(6)} %select_n.118), kind=kOutput, calls=%fused_computation.8.clone.1 | convolution fusion | flops 547356672 | bytes 9709572 | tf_op jit(solution)/shard_map/while/body/eval_jaxpr/igqp,pgd->igqd/dot_general | solution.py:84
  149.1 5.5 %bitcast_reduce_fusion.2 = (f32[128,16]{0,1:T(8,128)S(1)}, f32[1024,128,16]{1,0,2:T(8,128)}) fusion(pred[1024]{0:T(1024)(128)(4,1)S(1)} %add_compare_fusion.3, bf16[128,1,16,128]{3,0,2,1:T(8,128)(2,1)S(1)} %get-tuple-element.349, bf16[8,1024,2,1,128]{4,1,3,2,0:T(8,128)(2,1)} %get-tuple-element.346, s32[]{:T(128)S(6)} %select_n.118), kind=kOutput, calls=%fused_computation.1.clone.1 | convolution fusion | flops 543160320 | bytes 9184260 | tf_op jit(solution)/shard_map/while/body/eval_jaxpr/igqd,pgd->igqp/dot_general | solution.py:63
  155.3 5.8 %fusion.85 = f32[128,128,16]{1,0,2:T(8,128)S(1)} fusion(f32[1024,128,16]{1,0,2:T(8,128)} %get-tuple-element.304, f32[128,16]{0,1:T(8,128)S(1)} %max.47, pred[1024]{0:T(1024)(128)(4,1)S(1)} %add_compare_fusion.3, bf16[8,1024,2,1,128]{4,1,3,2,0:T(8,128)(2,1)} %get-tuple-element.346, s32[]{:T(128)S(6)} %select_n.118), kind=kOutput, calls=%fused_computation.8.clone.1 | convolution fusion | flops 547356672 | bytes 9709572 | tf_op jit(solution)/shard_map/while/body/eval_jaxpr/igqp,pgd->igqd/dot_general | solution.py:84
  169.1 5.5 %bitcast_reduce_fusion.2 = (f32[128,16]{0,1:T(8,128)S(1)}, f32[1024,128,16]{1,0,2:T(8,128)}) fusion(pred[1024]{0:T(1024)(128)(4,1)S(1)} %add_compare_fusion.3, bf16[128,1,16,128]{3,0,2,1:T(8,128)(2,1)S(1)} %get-tuple-element.349, bf16[8,1024,2,1,128]{4,1,3,2,0:T(8,128)(2,1)} %get-tuple-element.346, s32[]{:T(128)S(6)} %select_n.118), kind=kOutput, calls=%fused_computation.1.clone.1 | convolution fusion | flops 543160320 | bytes 9184260 | tf_op jit(solution)/shard_map/while/body/eval_jaxpr/igqd,pgd->igqp/dot_general | solution.py:63
  175.4 5.8 %fusion.85 = f32[128,128,16]{1,0,2:T(8,128)S(1)} fusion(f32[1024,128,16]{1,0,2:T(8,128)} %get-tuple-element.304, f32[128,16]{0,1:T(8,128)S(1)} %max.47, pred[1024]{0:T(1024)(128)(4,1)S(1)} %add_compare_fusion.3, bf16[8,1024,2,1,128]{4,1,3,2,0:T(8,128)(2,1)} %get-tuple-element.346, s32[]{:T(128)S(6)} %select_n.118), kind=kOutput, calls=%fused_computation.8.clone.1 | convolution fusion | flops 547356672 | bytes 9709572 | tf_op jit(solution)/shard_map/while/body/eval_jaxpr/igqp,pgd->igqd/dot_general | solution.py:84
  189.1 5.5 %bitcast_reduce_fusion.2 = (f32[128,16]{0,1:T(8,128)S(1)}, f32[1024,128,16]{1,0,2:T(8,128)}) fusion(pred[1024]{0:T(1024)(128)(4,1)S(1)} %add_compare_fusion.3, bf16[128,1,16,128]{3,0,2,1:T(8,128)(2,1)S(1)} %get-tuple-element.349, bf16[8,1024,2,1,128]{4,1,3,2,0:T(8,128)(2,1)} %get-tuple-element.346, s32[]{:T(128)S(6)} %select_n.118), kind=kOutput, calls=%fused_computation.1.clone.1 | convolution fusion | flops 543160320 | bytes 9184260 | tf_op jit(solution)/shard_map/while/body/eval_jaxpr/igqd,pgd->igqp/dot_general | solution.py:63
  195.4 5.8 %fusion.85 = f32[128,128,16]{1,0,2:T(8,128)S(1)} fusion(f32[1024,128,16]{1,0,2:T(8,128)} %get-tuple-element.304, f32[128,16]{0,1:T(8,128)S(1)} %max.47, pred[1024]{0:T(1024)(128)(4,1)S(1)} %add_compare_fusion.3, bf16[8,1024,2,1,128]{4,1,3,2,0:T(8,128)(2,1)} %get-tuple-element.346, s32[]{:T(128)S(6)} %select_n.118), kind=kOutput, calls=%fused_computation.8.clone.1 | convolution fusion | flops 547356672 | bytes 9709572 | tf_op jit(solution)/shard_map/while/body/eval_jaxpr/igqp,pgd->igqd/dot_general | solution.py:84
  209.2 5.5 %bitcast_reduce_fusion.2 = (f32[128,16]{0,1:T(8,128)S(1)}, f32[1024,128,16]{1,0,2:T(8,128)}) fusion(pred[1024]{0:T(1024)(128)(4,1)S(1)} %add_compare_fusion.3, bf16[128,1,16,128]{3,0,2,1:T(8,128)(2,1)S(1)} %get-tuple-element.349, bf16[8,1024,2,1,128]{4,1,3,2,0:T(8,128)(2,1)} %get-tuple-element.346, s32[]{:T(128)S(6)} %select_n.118), kind=kOutput, calls=%fused_computation.1.clone.1 | convolution fusion | flops 543160320 | bytes 9184260 | tf_op jit(solution)/shard_map/while/body/eval_jaxpr/igqd,pgd->igqp/dot_general | solution.py:63
  215.5 5.8 %fusion.85 = f32[128,128,16]{1,0,2:T(8,128)S(1)} fusion(f32[1024,128,16]{1,0,2:T(8,128)} %get-tuple-element.304, f32[128,16]{0,1:T(8,128)S(1)} %max.47, pred[1024]{0:T(1024)(128)(4,1)S(1)} %add_compare_fusion.3, bf16[8,1024,2,1,128]{4,1,3,2,0:T(8,128)(2,1)} %get-tuple-element.346, s32[]{:T(128)S(6)} %select_n.118), kind=kOutput, calls=%fused_computation.8.clone.1 | convolution fusion | flops 547356672 | bytes 9709572 | tf_op jit(solution)/shard_map/while/body/eval_jaxpr/igqp,pgd->igqd/dot_general | solution.py:84
  229.3 5.5 %bitcast_reduce_fusion.2 = (f32[128,16]{0,1:T(8,128)S(1)}, f32[1024,128,16]{1,0,2:T(8,128)}) fusion(pred[1024]{0:T(1024)(128)(4,1)S(1)} %add_compare_fusion.3, bf16[128,1,16,128]{3,0,2,1:T(8,128)(2,1)S(1)} %get-tuple-element.349, bf16[8,1024,2,1,128]{4,1,3,2,0:T(8,128)(2,1)} %get-tuple-element.346, s32[]{:T(128)S(6)} %select_n.118), kind=kOutput, calls=%fused_computation.1.clone.1 | convolution fusion | flops 543160320 | bytes 9184260 | tf_op jit(solution)/shard_map/while/body/eval_jaxpr/igqd,pgd->igqp/dot_general | solution.py:63
  235.5 5.8 %fusion.85 = f32[128,128,16]{1,0,2:T(8,128)S(1)} fusion(f32[1024,128,16]{1,0,2:T(8,128)} %get-tuple-element.304, f32[128,16]{0,1:T(8,128)S(1)} %max.47, pred[1024]{0:T(1024)(128)(4,1)S(1)} %add_compare_fusion.3, bf16[8,1024,2,1,128]{4,1,3,2,0:T(8,128)(2,1)} %get-tuple-element.346, s32[]{:T(128)S(6)} %select_n.118), kind=kOutput, calls=%fused_computation.8.clone.1 | convolution fusion | flops 547356672 | bytes 9709572 | tf_op jit(solution)/shard_map/while/body/eval_jaxpr/igqp,pgd->igqd/dot_general | solution.py:84
  245.5 4.8 %multiply_reduce_fusion = f32[128,16,128]{0,2,1:T(8,128)S(1)} fusion(f32[8,128,16,128]{1,3,2,0:T(8,128)} %get-tuple-element.146, f32[8,128,16]{1,2,0:T(8,128)S(1)} %get-tuple-element.224), kind=kLoop, calls=%fused_computation.46 | loop fusion | flops 3932160 | bytes 9502720 | tf_op jit(solution)/shard_map/reduce_sum | solution.py:108
  252.2 5.2 %all-to-all-start.2 = ((f32[4,32,2080]{2,1,0:T(8,128)}), f32[4,32,2080]{2,1,0:T(8,128)S(1)}, u32[]{:S(2)}, u32[]{:S(2)}) async-start(f32[4,32,2080]{2,1,0:T(8,128)} %concatenate.17), calls=%async_computation.2 | async-start | bytes 2228224 | tf_op jit(solution)/shard_map/all_to_all | solution.py:112
  258.7 13.1 %all-to-all-done.2 = f32[4,32,2080]{2,1,0:T(8,128)S(1)} async-done(((f32[4,32,2080]{2,1,0:T(8,128)}), f32[4,32,2080]{2,1,0:T(8,128)S(1)}, u32[]{:S(2)}, u32[]{:S(2)}) %all-to-all-start.2) | async-done | bytes 1064992 | tf_op jit(solution)/shard_map/all_to_all | solution.py:112
  (158 shorter events, 62.0 us)
Async XLA Ops:
  0.0 78.3 %copy-start = (bf16[32,128]{1,0:T(8,128)(2,1)S(1)}, bf16[32,128]{1,0:T(8,128)(2,1)}, u32[]{:S(2)}) copy-start(bf16[32,128]{1,0:T(8,128)(2,1)} %param.13) | copy-start | bytes 24580
  0.0 20.2 %all-to-all-start.1 = ((bf16[4,8,2048]{2,0,1:T(4,128)(2,1)}), bf16[4,8,2048]{2,0,1:T(4,128)(2,1)S(1)}, u32[]{:S(2)}, u32[]{:S(2)}) async-start(bf16[4,8,2048]{2,0,1:T(4,128)(2,1)} %bitcast.168), calls=%async_computation.1 | async-start | bytes 262144 | tf_op jit(solution)/shard_map/all_to_all | solution.py:41
  16.0 10.9 %copy-start.3 = (s32[8]{0:T(128)S(1)}, s32[8]{0:T(128)}, u32[]{:S(2)}) copy-start(s32[8]{0:T(128)} %param.17) | copy-start | bytes 100
  16.0 11.5 %copy-start.2 = (s32[8,128]{1,0:T(8,128)S(1)}, s32[8,128]{1,0:T(8,128)}, u32[]{:S(2)}) copy-start(s32[8,128]{1,0:T(8,128)} %param.15) | copy-start | bytes 12292
  20.2 58.3 %all-to-all-start = ((bf16[8,1024,256]{1,2,0:T(8,128)(2,1)}), bf16[8,1024,256]{1,2,0:T(8,128)(2,1)}, u32[]{:S(2)}, u32[]{:S(2)}) async-start(bf16[8,1024,256]{1,2,0:T(8,128)(2,1)} %pad_maximum_fusion), calls=%async_computation | async-start | bytes 8388608 | tf_op jit(solution)/shard_map/all_to_all | solution.py:45
  26.8 58.1 %copy-start.1 = (bf16[32,128]{1,0:T(8,128)(2,1)S(1)}, bf16[32,128]{1,0:T(8,128)(2,1)}, u32[]{:S(2)}) copy-start(bf16[32,128]{1,0:T(8,128)(2,1)} %param.14) | copy-start | bytes 24580
  95.1 5.9 %slice-start = ((s8[8388608]{0:T(1024)(128)(4,1)}), s8[4194304]{0:T(1024)(128)(4,1)S(1)}, s32[]{:S(2)}) async-start(s8[8388608]{0:T(1024)(128)(4,1)} %bitcast.160), calls=%async_computation.3 | async-start | bytes 8388608 | tf_op jit(solution)/shard_map/while
  95.2 5.9 %slice-start.1 = ((s8[8388608]{0:T(1024)(128)(4,1)}), s8[4194304]{0:T(1024)(128)(4,1)S(1)}, s32[]{:S(2)}) async-start(s8[8388608]{0:T(1024)(128)(4,1)} %bitcast.160), calls=%async_computation.4 | async-start | bytes 8388608 | tf_op jit(solution)/shard_map/while
  115.1 5.9 %slice-start = ((s8[8388608]{0:T(1024)(128)(4,1)}), s8[4194304]{0:T(1024)(128)(4,1)S(1)}, s32[]{:S(2)}) async-start(s8[8388608]{0:T(1024)(128)(4,1)} %bitcast.160), calls=%async_computation.3 | async-start | bytes 8388608 | tf_op jit(solution)/shard_map/while
  115.2 5.9 %slice-start.1 = ((s8[8388608]{0:T(1024)(128)(4,1)}), s8[4194304]{0:T(1024)(128)(4,1)S(1)}, s32[]{:S(2)}) async-start(s8[8388608]{0:T(1024)(128)(4,1)} %bitcast.160), calls=%async_computation.4 | async-start | bytes 8388608 | tf_op jit(solution)/shard_map/while
  135.2 5.9 %slice-start = ((s8[8388608]{0:T(1024)(128)(4,1)}), s8[4194304]{0:T(1024)(128)(4,1)S(1)}, s32[]{:S(2)}) async-start(s8[8388608]{0:T(1024)(128)(4,1)} %bitcast.160), calls=%async_computation.3 | async-start | bytes 8388608 | tf_op jit(solution)/shard_map/while
  135.3 5.9 %slice-start.1 = ((s8[8388608]{0:T(1024)(128)(4,1)}), s8[4194304]{0:T(1024)(128)(4,1)S(1)}, s32[]{:S(2)}) async-start(s8[8388608]{0:T(1024)(128)(4,1)} %bitcast.160), calls=%async_computation.4 | async-start | bytes 8388608 | tf_op jit(solution)/shard_map/while
  155.2 5.9 %slice-start = ((s8[8388608]{0:T(1024)(128)(4,1)}), s8[4194304]{0:T(1024)(128)(4,1)S(1)}, s32[]{:S(2)}) async-start(s8[8388608]{0:T(1024)(128)(4,1)} %bitcast.160), calls=%async_computation.3 | async-start | bytes 8388608 | tf_op jit(solution)/shard_map/while
  155.3 5.9 %slice-start.1 = ((s8[8388608]{0:T(1024)(128)(4,1)}), s8[4194304]{0:T(1024)(128)(4,1)S(1)}, s32[]{:S(2)}) async-start(s8[8388608]{0:T(1024)(128)(4,1)} %bitcast.160), calls=%async_computation.4 | async-start | bytes 8388608 | tf_op jit(solution)/shard_map/while
  175.3 5.9 %slice-start = ((s8[8388608]{0:T(1024)(128)(4,1)}), s8[4194304]{0:T(1024)(128)(4,1)S(1)}, s32[]{:S(2)}) async-start(s8[8388608]{0:T(1024)(128)(4,1)} %bitcast.160), calls=%async_computation.3 | async-start | bytes 8388608 | tf_op jit(solution)/shard_map/while
  175.4 5.9 %slice-start.1 = ((s8[8388608]{0:T(1024)(128)(4,1)}), s8[4194304]{0:T(1024)(128)(4,1)S(1)}, s32[]{:S(2)}) async-start(s8[8388608]{0:T(1024)(128)(4,1)} %bitcast.160), calls=%async_computation.4 | async-start | bytes 8388608 | tf_op jit(solution)/shard_map/while
  195.3 5.9 %slice-start = ((s8[8388608]{0:T(1024)(128)(4,1)}), s8[4194304]{0:T(1024)(128)(4,1)S(1)}, s32[]{:S(2)}) async-start(s8[8388608]{0:T(1024)(128)(4,1)} %bitcast.160), calls=%async_computation.3 | async-start | bytes 8388608 | tf_op jit(solution)/shard_map/while
  195.4 5.9 %slice-start.1 = ((s8[8388608]{0:T(1024)(128)(4,1)}), s8[4194304]{0:T(1024)(128)(4,1)S(1)}, s32[]{:S(2)}) async-start(s8[8388608]{0:T(1024)(128)(4,1)} %bitcast.160), calls=%async_computation.4 | async-start | bytes 8388608 | tf_op jit(solution)/shard_map/while
  215.4 5.9 %slice-start = ((s8[8388608]{0:T(1024)(128)(4,1)}), s8[4194304]{0:T(1024)(128)(4,1)S(1)}, s32[]{:S(2)}) async-start(s8[8388608]{0:T(1024)(128)(4,1)} %bitcast.160), calls=%async_computation.3 | async-start | bytes 8388608 | tf_op jit(solution)/shard_map/while
  215.5 5.9 %slice-start.1 = ((s8[8388608]{0:T(1024)(128)(4,1)}), s8[4194304]{0:T(1024)(128)(4,1)S(1)}, s32[]{:S(2)}) async-start(s8[8388608]{0:T(1024)(128)(4,1)} %bitcast.160), calls=%async_computation.4 | async-start | bytes 8388608 | tf_op jit(solution)/shard_map/while
  235.4 5.9 %slice-start = ((s8[8388608]{0:T(1024)(128)(4,1)}), s8[4194304]{0:T(1024)(128)(4,1)S(1)}, s32[]{:S(2)}) async-start(s8[8388608]{0:T(1024)(128)(4,1)} %bitcast.160), calls=%async_computation.3 | async-start | bytes 8388608 | tf_op jit(solution)/shard_map/while
  235.5 5.9 %slice-start.1 = ((s8[8388608]{0:T(1024)(128)(4,1)}), s8[4194304]{0:T(1024)(128)(4,1)S(1)}, s32[]{:S(2)}) async-start(s8[8388608]{0:T(1024)(128)(4,1)} %bitcast.160), calls=%async_computation.4 | async-start | bytes 8388608 | tf_op jit(solution)/shard_map/while
  245.5 11.9 %copy-start.4 = (s32[8]{0:T(128)S(1)}, s32[8]{0:T(128)}, u32[]{:S(2)}) copy-start(s32[8]{0:T(128)} %param.16) | copy-start | bytes 100
  252.2 19.5 %all-to-all-start.2 = ((f32[4,32,2080]{2,1,0:T(8,128)}), f32[4,32,2080]{2,1,0:T(8,128)S(1)}, u32[]{:S(2)}, u32[]{:S(2)}) async-start(f32[4,32,2080]{2,1,0:T(8,128)} %concatenate.17), calls=%async_computation.2 | async-start | bytes 2228224 | tf_op jit(solution)/shard_map/all_to_all | solution.py:112
where the time goes:
time: 275 us; the launch traced here: 273 us
  matrix products  103 us (37%)
  blocking collectives  47.9 us (17%)
  other arithmetic  36.8 us (13%)
  loops' own time  27.8 us (10%)
  local copies, waits for them, and re-layouts  23.5 us (9%)
  starting transfers between devices  21 us (8%)
  waiting for transfers between devices  13.1 us (5%)
    all_gather x1, blocking collectives, body(): query_block = lax.all_gather(by_head, 'rl', axis=0, tiled=True)  47.9 us
    dot_general x8, matrix products, one_group(): jnp.einsum('igqp,pgd->igqd', cache_weights.astype(jnp.bfloat16), block_va...  46.3 us
    dot_general x8, matrix products, one_group(): jnp.einsum('igqd,pgd->igqp', query_block, block_keys, preferred_element_t...  43.9 us
    another operation x1, loops' own time, body(): partials, log_totals = lax.map(one_group, jnp.arange(n_hi, dtype=jnp.int32))  27.8 us
    reduce_sum x16, other arithmetic, one_group(): totals = jnp.sum(cache_weights, axis=3) + jnp.sum(tree_weights, axis=3)  20.8 us
    all_to_all x1, waiting for transfers between devices, body(): lax.all_to_all(payload, 'rl', split_axis=0, concat_axis=0, tiled=True)  13.1 us
    dot_general x8, matrix products, one_group(): jnp.einsum('igqr,rgd->igqd', tree_weights.astype(jnp.bfloat16), local_tre...  10.8 us
    all_to_all x1, starting transfers between devices, body(): lax.all_to_all(queries, 'head', split_axis=1, concat_axis=0, tiled=True)  9.15 us
  transfers between devices with their start and end apart: 3, of which 1 were waited for; matrix products, arithmetic and copies ran while one was open for 6% of the time, Pallas kernels for 0%

commit v1 on v0

--- a/solution.py
+++ b/solution.py
@@ -4,11 +4,28 @@
 from jax import lax
 from jax.sharding import Mesh
 from jax.sharding import PartitionSpec as P
+from jax.lax import axis_index, axis_size, ppermute
 
 NH = 128
 KVH = 8
 HD = 128
 negative_fill = -1e30
+
+
+def _settle_modes(block_here, dim_at, arr):
+    carry, piece_now = (block_here.shape[:dim_at], block_here.shape[dim_at + 1 :])
+    carry_in = block_here.reshape(*carry, arr, -1, *piece_now)
+    all_values = jnp.moveaxis(carry_in, dim_at, 0)
+    return all_values
+
+
+def _produce_task(local_x, dim_no):
+    local_x = jnp.moveaxis(local_x, 0, dim_no)
+    t_next = local_x.shape
+    extra = local_x.reshape(
+        *t_next[:dim_no], t_next[dim_no] * t_next[dim_no + 1], *t_next[dim_no + 2 :]
+    )
+    return extra
 
 
 def ancestry(parents):
@@ -38,7 +55,22 @@
     heads_local = kv_local * group_size
     node_count = parents.shape[1]
     rows_owned = tree_keys.shape[0]
-    by_head = lax.all_to_all(queries, "head", split_axis=1, concat_axis=0, tiled=True)
+
+    def guide_slabs(matrix, block_in, point, net_axis):
+        clean = axis_size(net_axis)
+        high, upper = (clean, axis_index(net_axis))
+        g_now = _settle_modes(matrix, point, high)
+        shelf = [g_now[upper]]
+        for pp in range(1, high):
+            piece_out = g_now[upper ^ pp]
+            res = ppermute(piece_out, net_axis, [(j, j ^ pp) for j in range(high)])
+            shelf.append(res)
+        y2 = jnp.stack(shelf, axis=0)
+        g_now = y2[upper ^ jnp.arange(high)]
+        z_new = _produce_task(g_now, block_in)
+        return z_new
+
+    by_head = guide_slabs(queries, 0, 1, net_axis="head")
     query_block = lax.all_gather(by_head, "rl", axis=0, tiled=True)
     query_block = query_block.reshape(node_count, kv_local, group_size, HD)
     both = jnp.concatenate([cache_keys, cache_values], axis=2)

time: 275 us -> 266 us (0.967)
  blocking collectives: 47.9 us -> 28.1 us
  starting transfers between devices: 21 us -> 27.4 us
  waiting for transfers between devices: 13.1 us -> 17.1 us
    all_gather x1, blocking collectives: 47.9 us -> 28.1 us  [body(): query_block = lax.all_gather(by_head, 'rl', axis=0, tiled=True)]
    ppermute x0 -> x7, starting transfers between devices: none -> 14.8 us  [guide_slabs(): res = ppermute(piece_out, net_axis, [(j, j ^ pp) for j in range(high)])]
    all_to_all x1 -> x0, starting transfers between devices: 9.15 us -> none  [body(): lax.all_to_all(queries, 'head', split_axis=1, concat_axis=0, tiled=True)]
    ppermute x0 -> x7, waiting for transfers between devices: none -> 4.07 us  [guide_slabs(): res = ppermute(piece_out, net_axis, [(j, j ^ pp) for j in range(high)])]
    unnamed x12 -> x21, local copies, waits for them, and re-layouts: 6.81 us -> 6.93 us
  transfers between devices with their start and end apart: 3 -> 9, of which waited for: 1 -> 3; matrix products, arithmetic and copies ran while one was open for 6% -> 2% of each run, Pallas kernels for 0% -> 0%
where the time goes in v1:
time: 266 us; the launch traced here: 265 us
  matrix products  103 us (39%)
  other arithmetic  36.8 us (14%)
  blocking collectives  28.1 us (11%)
  loops' own time  27.8 us (10%)
  starting transfers between devices  27.4 us (10%)
  local copies, waits for them, and re-layouts  24.3 us (9%)
  waiting for transfers between devices  17.1 us (6%)
    dot_general x8, matrix products, one_group(): jnp.einsum('igqp,pgd->igqd', cache_weights.astype(jnp.bfloat16), block_va...  46.3 us
    dot_general x8, matrix products, one_group(): jnp.einsum('igqd,pgd->igqp', query_block, block_keys, preferred_element_t...  43.8 us
    all_gather x1, blocking collectives, body(): query_block = lax.all_gather(by_head, 'rl', axis=0, tiled=True)  28.1 us
    another operation x1, loops' own time, body(): partials, log_totals = lax.map(one_group, jnp.arange(n_hi, dtype=jnp.int32))  27.8 us
    reduce_sum x16, other arithmetic, one_group(): totals = jnp.sum(cache_weights, axis=3) + jnp.sum(tree_weights, axis=3)  20.8 us
    ppermute x7, starting transfers between devices, guide_slabs(): res = ppermute(piece_out, net_axis, [(j, j ^ pp) for j in range(high)])  14.8 us
    all_to_all x1, waiting for transfers between devices, body(): lax.all_to_all(payload, 'rl', split_axis=0, concat_axis=0, tiled=True)  13.1 us
    dot_general x8, matrix products, one_group(): jnp.einsum('igqr,rgd->igqd', tree_weights.astype(jnp.bfloat16), local_tre...  10.8 us
  transfers between devices with their start and end apart: 9, of which 3 were waited for; matrix products, arithmetic and copies ran while one was open for 2% of the time, Pallas kernels for 0%

profile of v1, /device:TPU:1, one launch (start us, length us, event | category | flops | bytes accessed | tf_op | source)
XLA Modules:
  0.0 265.1 jit_solution(8268169738429491089)
XLA Ops:
  11.0 7.5 %all-to-all-start = ((bf16[8,1024,256]{1,2,0:T(8,128)(2,1)}), bf16[8,1024,256]{1,2,0:T(8,128)(2,1)}, u32[]{:S(2)}, u32[]{:S(2)}) async-start(bf16[8,1024,256]{1,2,0:T(8,128)(2,1)} %pad_maximum_fusion), calls=%async_computation | async-start | bytes 8388608 | tf_op jit(solution)/shard_map/all_to_all | solution.py:77
  23.4 5.8 %collective-permute-start.3 = (bf16[4,2048]{1,0:T(4,128)(2,1)S(1)}, bf16[4,2048]{1,0:T(4,128)(2,1)S(1)}, u32[]{:S(2)}, u32[]{:S(2)}) collective-permute-start(bf16[4,2048]{1,0:T(4,128)(2,1)S(1)} %get-tuple-element.230), channel_id=1, source_target_pairs={{0,4},{1,5},{2,6},{3,7},{4,0},{5,1},{6,2},{7,3},{8,12},{9,13},{10,... | collective-permute-start | bytes 49160 | tf_op jit(solution)/shard_map/ppermute | solution.py:66
  41.3 28.1 %all_gather.3 = bf16[128,2048]{1,0:T(8,128)(2,1)S(1)} all-gather(bf16[32,2048]{1,0:T(8,128)(2,1)S(1)} %reshape.258), channel_id=1, replica_groups=mesh['rh'=8,'rl'=4,'head'=8] {'rl'}, dimensions={0}, use_global_device_ids=true | all-gather | bytes 655360 | tf_op jit(solution)/shard_map/all_gather | solution.py:74
  70.2 6.5 %copy.96 = bf16[8,1024,2,1,128]{4,1,3,2,0:T(8,128)(2,1)} copy(bf16[8,1024,2,1,128]{1,4,2,0,3:T(8,128)(2,1)} %bitcast.20) | data formatting | bytes 8388608 | tf_op jit(solution)/shard_map/while | solution.py:136
  76.7 160.4 %while.14 = (s32[]{:T(128)}, f32[8,128,16,128]{1,3,2,0:T(8,128)}, f32[8,128,16]{1,2,0:T(8,128)S(1)}, s32[8]{0:T(128)S(1)}, bf16[8,1024,2,1,128]{4,1,3,2,0:T(8,12...) while((s32[]{:T(128)}, f32[8,128,16,128]{1,3,2,0:T(8,128)}, ...), condition=%wide.region_5.6_spmd, body=%wide.region_0.5_spmd.sunk | while | flops 1119164416 | bytes 55485768 | solution.py:136
  80.6 5.5 %bitcast_reduce_fusion.2 = (f32[128,16]{0,1:T(8,128)S(1)}, f32[1024,128,16]{1,0,2:T(8,128)}) fusion(pred[1024]{0:T(1024)(128)(4,1)S(1)} %add_compare_fusion.3, bf16[128,1,16,128]{3,0,2,1:T(8,128)(2,1)S(1)} %get-tuple-element.356, bf16[8,1024,2,1,128]{4,1,3,2,0:T(8,128)(2,1)} %get-tuple-element.353, s32[]{:T(128)S(6)} %select_n.164), kind=kOutput, calls=%fused_computation.2.clone.1 | convolution fusion | flops 543160320 | bytes 9184260 | tf_op jit(solution)/shard_map/while/body/eval_jaxpr/igqd,pgd->igqp/dot_general | solution.py:95
  86.9 5.8 %fusion.85 = f32[128,128,16]{1,0,2:T(8,128)S(1)} fusion(f32[1024,128,16]{1,0,2:T(8,128)} %get-tuple-element.311, f32[128,16]{0,1:T(8,128)S(1)} %max.47, pred[1024]{0:T(1024)(128)(4,1)S(1)} %add_compare_fusion.3, bf16[8,1024,2,1,128]{4,1,3,2,0:T(8,128)(2,1)} %get-tuple-element.353, s32[]{:T(128)S(6)} %select_n.164), kind=kOutput, calls=%fused_computation.9.clone.1 | convolution fusion | flops 547356672 | bytes 9709572 | tf_op jit(solution)/shard_map/while/body/eval_jaxpr/igqp,pgd->igqd/dot_general | solution.py:116
  100.6 5.5 %bitcast_reduce_fusion.2 = (f32[128,16]{0,1:T(8,128)S(1)}, f32[1024,128,16]{1,0,2:T(8,128)}) fusion(pred[1024]{0:T(1024)(128)(4,1)S(1)} %add_compare_fusion.3, bf16[128,1,16,128]{3,0,2,1:T(8,128)(2,1)S(1)} %get-tuple-element.356, bf16[8,1024,2,1,128]{4,1,3,2,0:T(8,128)(2,1)} %get-tuple-element.353, s32[]{:T(128)S(6)} %select_n.164), kind=kOutput, calls=%fused_computation.2.clone.1 | convolution fusion | flops 543160320 | bytes 9184260 | tf_op jit(solution)/shard_map/while/body/eval_jaxpr/igqd,pgd->igqp/dot_general | solution.py:95
  106.9 5.8 %fusion.85 = f32[128,128,16]{1,0,2:T(8,128)S(1)} fusion(f32[1024,128,16]{1,0,2:T(8,128)} %get-tuple-element.311, f32[128,16]{0,1:T(8,128)S(1)} %max.47, pred[1024]{0:T(1024)(128)(4,1)S(1)} %add_compare_fusion.3, bf16[8,1024,2,1,128]{4,1,3,2,0:T(8,128)(2,1)} %get-tuple-element.353, s32[]{:T(128)S(6)} %select_n.164), kind=kOutput, calls=%fused_computation.9.clone.1 | convolution fusion | flops 547356672 | bytes 9709572 | tf_op jit(solution)/shard_map/while/body/eval_jaxpr/igqp,pgd->igqd/dot_general | solution.py:116
  120.7 5.5 %bitcast_reduce_fusion.2 = (f32[128,16]{0,1:T(8,128)S(1)}, f32[1024,128,16]{1,0,2:T(8,128)}) fusion(pred[1024]{0:T(1024)(128)(4,1)S(1)} %add_compare_fusion.3, bf16[128,1,16,128]{3,0,2,1:T(8,128)(2,1)S(1)} %get-tuple-element.356, bf16[8,1024,2,1,128]{4,1,3,2,0:T(8,128)(2,1)} %get-tuple-element.353, s32[]{:T(128)S(6)} %select_n.164), kind=kOutput, calls=%fused_computation.2.clone.1 | convolution fusion | flops 543160320 | bytes 9184260 | tf_op jit(solution)/shard_map/while/body/eval_jaxpr/igqd,pgd->igqp/dot_general | solution.py:95
  127.0 5.8 %fusion.85 = f32[128,128,16]{1,0,2:T(8,128)S(1)} fusion(f32[1024,128,16]{1,0,2:T(8,128)} %get-tuple-element.311, f32[128,16]{0,1:T(8,128)S(1)} %max.47, pred[1024]{0:T(1024)(128)(4,1)S(1)} %add_compare_fusion.3, bf16[8,1024,2,1,128]{4,1,3,2,0:T(8,128)(2,1)} %get-tuple-element.353, s32[]{:T(128)S(6)} %select_n.164), kind=kOutput, calls=%fused_computation.9.clone.1 | convolution fusion | flops 547356672 | bytes 9709572 | tf_op jit(solution)/shard_map/while/body/eval_jaxpr/igqp,pgd->igqd/dot_general | solution.py:116
  140.8 5.5 %bitcast_reduce_fusion.2 = (f32[128,16]{0,1:T(8,128)S(1)}, f32[1024,128,16]{1,0,2:T(8,128)}) fusion(pred[1024]{0:T(1024)(128)(4,1)S(1)} %add_compare_fusion.3, bf16[128,1,16,128]{3,0,2,1:T(8,128)(2,1)S(1)} %get-tuple-element.356, bf16[8,1024,2,1,128]{4,1,3,2,0:T(8,128)(2,1)} %get-tuple-element.353, s32[]{:T(128)S(6)} %select_n.164), kind=kOutput, calls=%fused_computation.2.clone.1 | convolution fusion | flops 543160320 | bytes 9184260 | tf_op jit(solution)/shard_map/while/body/eval_jaxpr/igqd,pgd->igqp/dot_general | solution.py:95
  147.0 5.8 %fusion.85 = f32[128,128,16]{1,0,2:T(8,128)S(1)} fusion(f32[1024,128,16]{1,0,2:T(8,128)} %get-tuple-element.311, f32[128,16]{0,1:T(8,128)S(1)} %max.47, pred[1024]{0:T(1024)(128)(4,1)S(1)} %add_compare_fusion.3, bf16[8,1024,2,1,128]{4,1,3,2,0:T(8,128)(2,1)} %get-tuple-element.353, s32[]{:T(128)S(6)} %select_n.164), kind=kOutput, calls=%fused_computation.9.clone.1 | convolution fusion | flops 547356672 | bytes 9709572 | tf_op jit(solution)/shard_map/while/body/eval_jaxpr/igqp,pgd->igqd/dot_general | solution.py:116
  160.8 5.5 %bitcast_reduce_fusion.2 = (f32[128,16]{0,1:T(8,128)S(1)}, f32[1024,128,16]{1,0,2:T(8,128)}) fusion(pred[1024]{0:T(1024)(128)(4,1)S(1)} %add_compare_fusion.3, bf16[128,1,16,128]{3,0,2,1:T(8,128)(2,1)S(1)} %get-tuple-element.356, bf16[8,1024,2,1,128]{4,1,3,2,0:T(8,128)(2,1)} %get-tuple-element.353, s32[]{:T(128)S(6)} %select_n.164), kind=kOutput, calls=%fused_computation.2.clone.1 | convolution fusion | flops 543160320 | bytes 9184260 | tf_op jit(solution)/shard_map/while/body/eval_jaxpr/igqd,pgd->igqp/dot_general | solution.py:95
  167.1 5.8 %fusion.85 = f32[128,128,16]{1,0,2:T(8,128)S(1)} fusion(f32[1024,128,16]{1,0,2:T(8,128)} %get-tuple-element.311, f32[128,16]{0,1:T(8,128)S(1)} %max.47, pred[1024]{0:T(1024)(128)(4,1)S(1)} %add_compare_fusion.3, bf16[8,1024,2,1,128]{4,1,3,2,0:T(8,128)(2,1)} %get-tuple-element.353, s32[]{:T(128)S(6)} %select_n.164), kind=kOutput, calls=%fused_computation.9.clone.1 | convolution fusion | flops 547356672 | bytes 9709572 | tf_op jit(solution)/shard_map/while/body/eval_jaxpr/igqp,pgd->igqd/dot_general | solution.py:116
  180.8 5.5 %bitcast_reduce_fusion.2 = (f32[128,16]{0,1:T(8,128)S(1)}, f32[1024,128,16]{1,0,2:T(8,128)}) fusion(pred[1024]{0:T(1024)(128)(4,1)S(1)} %add_compare_fusion.3, bf16[128,1,16,128]{3,0,2,1:T(8,128)(2,1)S(1)} %get-tuple-element.356, bf16[8,1024,2,1,128]{4,1,3,2,0:T(8,128)(2,1)} %get-tuple-element.353, s32[]{:T(128)S(6)} %select_n.164), kind=kOutput, calls=%fused_computation.2.clone.1 | convolution fusion | flops 543160320 | bytes 9184260 | tf_op jit(solution)/shard_map/while/body/eval_jaxpr/igqd,pgd->igqp/dot_general | solution.py:95
  187.1 5.8 %fusion.85 = f32[128,128,16]{1,0,2:T(8,128)S(1)} fusion(f32[1024,128,16]{1,0,2:T(8,128)} %get-tuple-element.311, f32[128,16]{0,1:T(8,128)S(1)} %max.47, pred[1024]{0:T(1024)(128)(4,1)S(1)} %add_compare_fusion.3, bf16[8,1024,2,1,128]{4,1,3,2,0:T(8,128)(2,1)} %get-tuple-element.353, s32[]{:T(128)S(6)} %select_n.164), kind=kOutput, calls=%fused_computation.9.clone.1 | convolution fusion | flops 547356672 | bytes 9709572 | tf_op jit(solution)/shard_map/while/body/eval_jaxpr/igqp,pgd->igqd/dot_general | solution.py:116
  200.9 5.5 %bitcast_reduce_fusion.2 = (f32[128,16]{0,1:T(8,128)S(1)}, f32[1024,128,16]{1,0,2:T(8,128)}) fusion(pred[1024]{0:T(1024)(128)(4,1)S(1)} %add_compare_fusion.3, bf16[128,1,16,128]{3,0,2,1:T(8,128)(2,1)S(1)} %get-tuple-element.356, bf16[8,1024,2,1,128]{4,1,3,2,0:T(8,128)(2,1)} %get-tuple-element.353, s32[]{:T(128)S(6)} %select_n.164), kind=kOutput, calls=%fused_computation.2.clone.1 | convolution fusion | flops 543160320 | bytes 9184260 | tf_op jit(solution)/shard_map/while/body/eval_jaxpr/igqd,pgd->igqp/dot_general | solution.py:95
  207.2 5.8 %fusion.85 = f32[128,128,16]{1,0,2:T(8,128)S(1)} fusion(f32[1024,128,16]{1,0,2:T(8,128)} %get-tuple-element.311, f32[128,16]{0,1:T(8,128)S(1)} %max.47, pred[1024]{0:T(1024)(128)(4,1)S(1)} %add_compare_fusion.3, bf16[8,1024,2,1,128]{4,1,3,2,0:T(8,128)(2,1)} %get-tuple-element.353, s32[]{:T(128)S(6)} %select_n.164), kind=kOutput, calls=%fused_computation.9.clone.1 | convolution fusion | flops 547356672 | bytes 9709572 | tf_op jit(solution)/shard_map/while/body/eval_jaxpr/igqp,pgd->igqd/dot_general | solution.py:116
  220.9 5.5 %bitcast_reduce_fusion.2 = (f32[128,16]{0,1:T(8,128)S(1)}, f32[1024,128,16]{1,0,2:T(8,128)}) fusion(pred[1024]{0:T(1024)(128)(4,1)S(1)} %add_compare_fusion.3, bf16[128,1,16,128]{3,0,2,1:T(8,128)(2,1)S(1)} %get-tuple-element.356, bf16[8,1024,2,1,128]{4,1,3,2,0:T(8,128)(2,1)} %get-tuple-element.353, s32[]{:T(128)S(6)} %select_n.164), kind=kOutput, calls=%fused_computation.2.clone.1 | convolution fusion | flops 543160320 | bytes 9184260 | tf_op jit(solution)/shard_map/while/body/eval_jaxpr/igqd,pgd->igqp/dot_general | solution.py:95
  227.2 5.8 %fusion.85 = f32[128,128,16]{1,0,2:T(8,128)S(1)} fusion(f32[1024,128,16]{1,0,2:T(8,128)} %get-tuple-element.311, f32[128,16]{0,1:T(8,128)S(1)} %max.47, pred[1024]{0:T(1024)(128)(4,1)S(1)} %add_compare_fusion.3, bf16[8,1024,2,1,128]{4,1,3,2,0:T(8,128)(2,1)} %get-tuple-element.353, s32[]{:T(128)S(6)} %select_n.164), kind=kOutput, calls=%fused_computation.9.clone.1 | convolution fusion | flops 547356672 | bytes 9709572 | tf_op jit(solution)/shard_map/while/body/eval_jaxpr/igqp,pgd->igqd/dot_general | solution.py:116
  237.2 4.8 %multiply_reduce_fusion = f32[128,16,128]{0,2,1:T(8,128)S(1)} fusion(f32[8,128,16,128]{1,3,2,0:T(8,128)} %get-tuple-element.146, f32[8,128,16]{1,2,0:T(8,128)S(1)} %get-tuple-element.224), kind=kLoop, calls=%fused_computation.47 | loop fusion | flops 3932160 | bytes 9502720 | tf_op jit(solution)/shard_map/reduce_sum | solution.py:140
  243.9 5.2 %all-to-all-start.1 = ((f32[4,32,2080]{2,1,0:T(8,128)}), f32[4,32,2080]{2,1,0:T(8,128)S(1)}, u32[]{:S(2)}, u32[]{:S(2)}) async-start(f32[4,32,2080]{2,1,0:T(8,128)} %concatenate.17), calls=%async_computation.1 | async-start | bytes 2228224 | tf_op jit(solution)/shard_map/all_to_all | solution.py:144
  250.3 13.1 %all-to-all-done.1 = f32[4,32,2080]{2,1,0:T(8,128)S(1)} async-done(((f32[4,32,2080]{2,1,0:T(8,128)}), f32[4,32,2080]{2,1,0:T(8,128)S(1)}, u32[]{:S(2)}, u32[]{:S(2)}) %all-to-all-start.1) | async-done | bytes 1064992 | tf_op jit(solution)/shard_map/all_to_all | solution.py:144
  (184 shorter events, 75.9 us)
Async XLA Ops:
  0.0 70.0 %copy-start = (bf16[32,128]{1,0:T(8,128)(2,1)S(1)}, bf16[32,128]{1,0:T(8,128)(2,1)}, u32[]{:S(2)}) copy-start(bf16[32,128]{1,0:T(8,128)(2,1)} %param.13) | copy-start | bytes 24580
  6.8 11.8 %copy-start.1 = (bf16[4,16384]{1,0:T(4,128)(2,1)S(1)}, bf16[4,16384]{1,0:T(4,128)(2,1)}, u32[]{:S(2)}) copy-start(bf16[4,16384]{1,0:T(4,128)(2,1)} %param.10) | copy-start | bytes 393220
  6.8 22.4 %copy-start.3 = (s32[8,128]{1,0:T(8,128)S(1)}, s32[8,128]{1,0:T(8,128)}, u32[]{:S(2)}) copy-start(s32[8,128]{1,0:T(8,128)} %param.15) | copy-start | bytes 12292
  6.8 24.6 %copy-start.4 = (s32[8]{0:T(128)S(1)}, s32[8]{0:T(128)}, u32[]{:S(2)}) copy-start(s32[8]{0:T(128)} %param.17) | copy-start | bytes 100
  11.0 59.2 %all-to-all-start = ((bf16[8,1024,256]{1,2,0:T(8,128)(2,1)}), bf16[8,1024,256]{1,2,0:T(8,128)(2,1)}, u32[]{:S(2)}, u32[]{:S(2)}) async-start(bf16[8,1024,256]{1,2,0:T(8,128)(2,1)} %pad_maximum_fusion), calls=%async_computation | async-start | bytes 8388608 | tf_op jit(solution)/shard_map/all_to_all | solution.py:77
  18.5 58.1 %copy-start.2 = (bf16[32,128]{1,0:T(8,128)(2,1)S(1)}, bf16[32,128]{1,0:T(8,128)(2,1)}, u32[]{:S(2)}) copy-start(bf16[32,128]{1,0:T(8,128)(2,1)} %param.14) | copy-start | bytes 24580
  18.6 13.5 %collective-permute-start = (bf16[4,2048]{1,0:T(4,128)(2,1)S(1)}, bf16[4,2048]{1,0:T(4,128)(2,1)S(1)}, u32[]{:S(2)}, u32[]{:S(2)}) collective-permute-start(bf16[4,2048]{1,0:T(4,128)(2,1)S(1)} %get-tuple-element.233), channel_id=1, source_target_pairs={{0,1},{1,0},{2,3},{3,2},{4,5},{5,4},{6,7},{7,6},{8,9},{9,8},{10,11... | collective-permute-start | bytes 49160 | tf_op jit(solution)/shard_map/ppermute | solution.py:66
  20.4 15.9 %collective-permute-start.1 = (bf16[4,2048]{1,0:T(4,128)(2,1)S(1)}, bf16[4,2048]{1,0:T(4,128)(2,1)S(1)}, u32[]{:S(2)}, u32[]{:S(2)}) collective-permute-start(bf16[4,2048]{1,0:T(4,128)(2,1)S(1)} %get-tuple-element.232), channel_id=1, source_target_pairs={{0,2},{1,3},{2,0},{3,1},{4,6},{5,7},{6,4},{7,5},{8,10},{9,11},{10,... | collective-permute-start | bytes 49160 | tf_op jit(solution)/shard_map/ppermute | solution.py:66
  23.4 13.0 %collective-permute-start.2 = (bf16[4,2048]{1,0:T(4,128)(2,1)S(1)}, bf16[4,2048]{1,0:T(4,128)(2,1)S(1)}, u32[]{:S(2)}, u32[]{:S(2)}) collective-permute-start(bf16[4,2048]{1,0:T(4,128)(2,1)S(1)} %get-tuple-element.231), channel_id=1, source_target_pairs={{0,3},{1,2},{2,1},{3,0},{4,7},{5,6},{6,5},{7,4},{8,11},{9,10},{10,... | collective-permute-start | bytes 49160 | tf_op jit(solution)/shard_map/ppermute | solution.py:66
  23.4 13.1 %collective-permute-start.3 = (bf16[4,2048]{1,0:T(4,128)(2,1)S(1)}, bf16[4,2048]{1,0:T(4,128)(2,1)S(1)}, u32[]{:S(2)}, u32[]{:S(2)}) collective-permute-start(bf16[4,2048]{1,0:T(4,128)(2,1)S(1)} %get-tuple-element.230), channel_id=1, source_target_pairs={{0,4},{1,5},{2,6},{3,7},{4,0},{5,1},{6,2},{7,3},{8,12},{9,13},{10,... | collective-permute-start | bytes 49160 | tf_op jit(solution)/shard_map/ppermute | solution.py:66
  29.2 7.3 %collective-permute-start.4 = (bf16[4,2048]{1,0:T(4,128)(2,1)S(1)}, bf16[4,2048]{1,0:T(4,128)(2,1)S(1)}, u32[]{:S(2)}, u32[]{:S(2)}) collective-permute-start(bf16[4,2048]{1,0:T(4,128)(2,1)S(1)} %get-tuple-element.229), channel_id=1, source_target_pairs={{0,5},{1,4},{2,7},{3,6},{4,1},{5,0},{6,3},{7,2},{8,13},{9,12},{10,... | collective-permute-start | bytes 49160 | tf_op jit(solution)/shard_map/ppermute | solution.py:66
  32.1 5.8 %collective-permute-start.5 = (bf16[4,2048]{1,0:T(4,128)(2,1)S(1)}, bf16[4,2048]{1,0:T(4,128)(2,1)S(1)}, u32[]{:S(2)}, u32[]{:S(2)}) collective-permute-start(bf16[4,2048]{1,0:T(4,128)(2,1)S(1)} %get-tuple-element.228), channel_id=1, source_target_pairs={{0,6},{1,7},{2,4},{3,5},{4,2},{5,3},{6,0},{7,1},{8,14},{9,15},{10,... | collective-permute-start | bytes 49160 | tf_op jit(solution)/shard_map/ppermute | solution.py:66
  36.3 4.3 %collective-permute-start.6 = (bf16[4,2048]{1,0:T(4,128)(2,1)S(1)}, bf16[4,2048]{1,0:T(4,128)(2,1)S(1)}, u32[]{:S(2)}, u32[]{:S(2)}) collective-permute-start(bf16[4,2048]{1,0:T(4,128)(2,1)S(1)} %get-tuple-element.227), channel_id=1, source_target_pairs={{0,7},{1,6},{2,5},{3,4},{4,3},{5,2},{6,1},{7,0},{8,15},{9,14},{10,... | collective-permute-start | bytes 49160 | tf_op jit(solution)/shard_map/ppermute | solution.py:66
  86.8 5.9 %slice-start = ((s8[8388608]{0:T(1024)(128)(4,1)}), s8[4194304]{0:T(1024)(128)(4,1)S(1)}, s32[]{:S(2)}) async-start(s8[8388608]{0:T(1024)(128)(4,1)} %bitcast.200), calls=%async_computation.2 | async-start | bytes 8388608 | tf_op jit(solution)/shard_map/while
  86.9 5.9 %slice-start.1 = ((s8[8388608]{0:T(1024)(128)(4,1)}), s8[4194304]{0:T(1024)(128)(4,1)S(1)}, s32[]{:S(2)}) async-start(s8[8388608]{0:T(1024)(128)(4,1)} %bitcast.200), calls=%async_computation.3 | async-start | bytes 8388608 | tf_op jit(solution)/shard_map/while
  106.8 5.9 %slice-start = ((s8[8388608]{0:T(1024)(128)(4,1)}), s8[4194304]{0:T(1024)(128)(4,1)S(1)}, s32[]{:S(2)}) async-start(s8[8388608]{0:T(1024)(128)(4,1)} %bitcast.200), calls=%async_computation.2 | async-start | bytes 8388608 | tf_op jit(solution)/shard_map/while
  126.9 5.9 %slice-start = ((s8[8388608]{0:T(1024)(128)(4,1)}), s8[4194304]{0:T(1024)(128)(4,1)S(1)}, s32[]{:S(2)}) async-start(s8[8388608]{0:T(1024)(128)(4,1)} %bitcast.200), calls=%async_computation.2 | async-start | bytes 8388608 | tf_op jit(solution)/shard_map/while
  146.9 5.9 %slice-start = ((s8[8388608]{0:T(1024)(128)(4,1)}), s8[4194304]{0:T(1024)(128)(4,1)S(1)}, s32[]{:S(2)}) async-start(s8[8388608]{0:T(1024)(128)(4,1)} %bitcast.200), calls=%async_computation.2 | async-start | bytes 8388608 | tf_op jit(solution)/shard_map/while
  167.0 5.9 %slice-start = ((s8[8388608]{0:T(1024)(128)(4,1)}), s8[4194304]{0:T(1024)(128)(4,1)S(1)}, s32[]{:S(2)}) async-start(s8[8388608]{0:T(1024)(128)(4,1)} %bitcast.200), calls=%async_computation.2 | async-start | bytes 8388608 | tf_op jit(solution)/shard_map/while
  187.0 5.9 %slice-start = ((s8[8388608]{0:T(1024)(128)(4,1)}), s8[4194304]{0:T(1024)(128)(4,1)S(1)}, s32[]{:S(2)}) async-start(s8[8388608]{0:T(1024)(128)(4,1)} %bitcast.200), calls=%async_computation.2 | async-start | bytes 8388608 | tf_op jit(solution)/shard_map/while
  207.1 5.9 %slice-start = ((s8[8388608]{0:T(1024)(128)(4,1)}), s8[4194304]{0:T(1024)(128)(4,1)S(1)}, s32[]{:S(2)}) async-start(s8[8388608]{0:T(1024)(128)(4,1)} %bitcast.200), calls=%async_computation.2 | async-start | bytes 8388608 | tf_op jit(solution)/shard_map/while
  227.1 5.9 %slice-start = ((s8[8388608]{0:T(1024)(128)(4,1)}), s8[4194304]{0:T(1024)(128)(4,1)S(1)}, s32[]{:S(2)}) async-start(s8[8388608]{0:T(1024)(128)(4,1)} %bitcast.200), calls=%async_computation.2 | async-start | bytes 8388608 | tf_op jit(solution)/shard_map/while
  237.2 11.9 %copy-start.5 = (s32[8]{0:T(128)S(1)}, s32[8]{0:T(128)}, u32[]{:S(2)}) copy-start(s32[8]{0:T(128)} %param.16) | copy-start | bytes 100
  243.9 19.5 %all-to-all-start.1 = ((f32[4,32,2080]{2,1,0:T(8,128)}), f32[4,32,2080]{2,1,0:T(8,128)S(1)}, u32[]{:S(2)}, u32[]{:S(2)}) async-start(f32[4,32,2080]{2,1,0:T(8,128)} %concatenate.17), calls=%async_computation.1 | async-start | bytes 2228224 | tf_op jit(solution)/shard_map/all_to_all | solution.py:144
  (7 other events, 41.0 us)
